TPU v7x, 32 devices: a whole 2x2x4 slice. The times are simulated.
32 devices in a mesh: region: 8 (over z, core), state: 4 (over y, x).
Axes of the slice: x: 2, y: 2, z: 4, core: 2. Of those that a mesh axis runs over, the one named last changes fastest.
Arguments:
- state_anom: float32 [8, 16, 256, 512], P('region', 'state'), may hold values from -6 to 6
- obs_anom: float32 [8, 256, 512], P('region', 'state'), may hold values from -6 to 6
- obs_weight: float32 [8, 256, 512], P('region', 'state'), may hold values from -6 to 6
- obs_cell: int32 [8, 256], P('region', 'state'), may hold values from 0 to 255, as said below
- sector_of: int32 [8], replicated, may hold values from 0 to 7, as said below
Outputs:
- increment: float32 [8, 16, 256, 512], P('region', 'state')
Inputs may be any that keep to these rules, and one draw needn't show every extreme that they name: `obs_cell`: each entry is lon * 8 + lat with lon in 0..31 and lat in 0..7. Within each aligned block of 64 entries along the observation dimension the entries do not decrease; in each such block between 8 and 16 entries have lon < 8, and between 8 and 16 have lon >= 24; the bound 16 is reached on both sides in every draw. `sector_of`: A permutation: every region holds a different sector.
All inputs are finite; a program needn't handle non-finite values.
Results may differ from a plain program's by a relative error of at most 0.0003.
Values sent between devices are 32-bit elements; how exact they have to be, the bound alone decides.
No kernel may reach another device: no remote copies, remote signals or barrier semaphores. Data moves between devices by JAX's collectives and lax.ppermute only.
A program may use at most 64 MiB of HBM per device.

v0:
```python
import jax
import jax.numpy as jnp
from jax import lax
from jax.sharding import PartitionSpec as P

SECT_W = 32
LAT = 8
HALF = 4
CAP = 16
COLS = 256


def gaspari(scaled):
    inside = scaled * scaled * (scaled * (scaled * (0.5 - 0.25 * scaled) + 0.625) - 5.0 / 3.0) + 1.0
    floored = jnp.maximum(scaled, 1.0)
    outside = (
        scaled * (scaled * (scaled * (scaled * (scaled / 12.0 - 0.5) + 0.625) + 5.0 / 3.0) - 5.0)
        + 4.0
        - 2.0 / (3.0 * floored)
    )
    return jnp.where(scaled <= 1.0, inside, jnp.where(scaled < 2.0, outside, 0.0))


def taper_tile(state_cells, obs_cells, lon_span):
    state_lon = state_cells // LAT
    state_lat = state_cells % LAT
    obs_lon = obs_cells // LAT
    obs_lat = obs_cells % LAT
    lon_gap = state_lon[:, None] - obs_lon[None, :]
    lon_gap = (lon_gap + lon_span + lon_span // 2) % lon_span - lon_span // 2
    lat_gap = state_lat[:, None] - obs_lat[None, :]
    scaled = jnp.sqrt((lon_gap * lon_gap + lat_gap * lat_gap).astype(jnp.float32)) / HALF
    return gaspari(scaled)


def add_block(flat_state, state_cells, pieces, lon_span):
    piece_anom, piece_weight, piece_cells = pieces
    covar = jnp.einsum("rm,pm->rp", flat_state, piece_anom, precision=lax.Precision.HIGHEST)
    columns = state_cells.shape[0]
    levels_here = flat_state.shape[0] // columns
    tile = taper_tile(state_cells, piece_cells, lon_span) / (flat_state.shape[1] - 1)
    covar = (covar.reshape(levels_here, columns, -1) * tile[None]).reshape(flat_state.shape[0], -1)
    return jnp.dot(covar, piece_weight, precision=lax.Precision.HIGHEST)


def on_device(state_anom, obs_anom, obs_weight, obs_cell, sector_of):
    regions = lax.axis_size("region")
    lon_span = regions * SECT_W
    region_ids = jnp.arange(regions, dtype=jnp.int32)
    my_region = lax.axis_index("region")
    my_sector = jnp.sum(jnp.where(region_ids == my_region, sector_of, 0))
    left_region = jnp.sum(
        jnp.where(sector_of == (my_sector + regions - 1) % regions, region_ids, 0)
    )
    right_region = jnp.sum(jnp.where(sector_of == (my_sector + 1) % regions, region_ids, 0))
    own_anom = obs_anom[0]
    own_weight = obs_weight[0]
    own_cells = obs_cell[0] + my_sector * (SECT_W * LAT)
    count = own_anom.shape[0]
    low_set = (own_anom[:CAP], own_weight[:CAP], own_cells[:CAP])
    high_set = (own_anom[count - CAP :], own_weight[count - CAP :], own_cells[count - CAP :])
    to_left = region_ids == left_region
    to_right = region_ids == right_region

    def place(first, second):
        shaped = (regions,) + (1,) * first.ndim
        return jnp.where(to_left.reshape(shaped), first[None], 0) + jnp.where(
            to_right.reshape(shaped), second[None], 0
        )

    slotted = (
        lax.all_to_all(
            place(low_set[0], high_set[0]), "region", split_axis=0, concat_axis=0, tiled=True
        ),
        lax.all_to_all(
            place(low_set[1], high_set[1]), "region", split_axis=0, concat_axis=0, tiled=True
        ),
        lax.all_to_all(
            place(low_set[2], high_set[2]), "region", split_axis=0, concat_axis=0, tiled=True
        ),
    )
    from_left = tuple(
        (lax.dynamic_index_in_dim(pieces, left_region, 0, keepdims=False) for pieces in slotted)
    )
    from_right = tuple(
        (lax.dynamic_index_in_dim(pieces, right_region, 0, keepdims=False) for pieces in slotted)
    )
    halo_set = tuple(
        (
            jnp.concatenate([left_part, right_part], axis=0)
            for left_part, right_part in zip(from_left, from_right)
        )
    )
    flat_state = state_anom[0].reshape(-1, state_anom.shape[-1])
    state_cells = my_sector * (SECT_W * LAT) + jnp.arange(COLS, dtype=jnp.int32)
    joined = tuple(
        (
            jnp.concatenate([own_part, halo_part], axis=0)
            for own_part, halo_part in zip((own_anom, own_weight, own_cells), halo_set)
        )
    )
    total = add_block(
        flat_state,
        state_cells,
        (
            lax.all_gather(joined[0], "state", axis=0, tiled=True),
            lax.all_gather(joined[1], "state", axis=0, tiled=True),
            lax.all_gather(joined[2], "state", axis=0, tiled=True),
        ),
        lon_span,
    )
    return total.reshape(state_anom.shape)


def solution(mesh):
    in_specs = (
        P("region", "state", None, None),
        P("region", "state", None),
        P("region", "state", None),
        P("region", "state"),
        P(),
    )
    out_specs = P("region", "state", None, None)
    return jax.shard_map(
        on_device, mesh=mesh, in_specs=in_specs, out_specs=out_specs, check_vma=False
    )
```

profile of v0, /device:TPU:0, one launch (start us, length us, event | category | flops | bytes accessed | tf_op | source)
XLA Modules:
  0.0 79.8 jit_solution(260493578877022644)
XLA Ops:
  0.0 0.0 copy-start
  0.0 1.4 %fusion.13 = s32[]{:T(128)} fusion(s32[8]{0:T(128)} %param.9, s32[]{:T(128)S(6)} %axis_index.15), kind=kLoop, calls=%fused_computation.55 | loop fusion | flops 23 | bytes 40 | tf_op jit(solution)/shard_map/reduce_sum | solution.py:51
  3.4 0.7 broadcast_add_fusion
  4.1 0.1 slice_bitcast_fusion.5
  4.2 1.4 %fusion.15 = (s32[]{:T(128)}, s32[]{:T(128)}) fusion(s32[8]{0:T(128)} %param.9, s32[]{:T(128)S(6)} %select_n.127, s32[]{:T(128)S(6)} %select_n.124), kind=kLoop, calls=%fused_computation.57 | loop fusion | flops 46 | bytes 48 | tf_op jit(solution)/shard_map/reduce_sum | solution.py:55
  5.5 1.2 %iota_compare_fusion = (pred[8]{0:T(512)(128)(4,1)S(1)}, pred[8]{0:T(512)(128)(4,1)S(1)}) fusion(s32[]{:T(128)} %get-tuple-element.5, s32[]{:T(128)} %get-tuple-element.6), kind=kLoop, calls=%fused_computation.62 | loop fusion | flops 16 | bytes 24 | tf_op jit(solution)/shard_map/eq | solution.py:63
  6.8 0.7 fusion.8
  7.4 6.4 %all-to-all-start.1 = ((s32[8,1,16]{2,1,0:T(1,128)}), s32[8,1,16]{2,1,0:T(1,128)S(1)}, u32[]{:S(2)}, u32[]{:S(2)}) async-start(s32[8,1,16]{2,1,0:T(1,128)} %fusion.8), calls=%async_computation.1 | async-start | bytes 8192 | tf_op jit(solution)/shard_map/all_to_all | solution.py:78
  13.8 0.7 fusion.19
  14.5 0.8 %slice_bitcast_fusion.1 = (f32[16,512]{1,0:T(8,128)S(1)}, f32[16,512]{1,0:T(8,128)S(1)}, f32[16,512]{1,0:T(8,128)S(1)}, f32[16,512]{1,0:T(8,128)S(1)}) fusion(f32[1,64,512]{2,1,0:T(8,128)} %param.7, f32[1,64,512]{2,1,0:T(8,128)} %param.6), kind=kLoop, calls=%fused_computation.25 | loop fusion | bytes 262144 | tf_op jit(solution)/shard_map/jit(_where)/broadcast_in_dim | solution.py:67
  15.3 0.9 %select_add_fusion = (f32[8,16,512]{2,1,0:T(8,128)}, f32[8,16,512]{2,1,0:T(8,128)}) fusion(f32[16,512]{1,0:T(8,128)S(1)} %get-tuple-element.12, f32[16,512]{1,0:T(8,128)S(1)} %get-tuple-element.11, pred[8]{0:T(512)(128)(4,1)S(1)} %get-tuple-element.25, pred[8]{0:T(512)(128)(4,1)S(1)} %get-tuple-element.26, f32[16,512]{1,0:T(8,128)S(1)} %get-tuple-element.27, ...), kind=kLoop, calls=%fused_computation.18 | loop fusion | flops 393216 | bytes 655376 | tf_op jit(solution)/shard_map/add | solution.py:67
  20.0 1.3 %dynamic-slice.2 = u32[1]{0:T(128)} dynamic-slice(u32[32]{0:T(128)} %constant.145, u32[]{:T(128)S(6)} %add.195), dynamic_slice_sizes={1} | dynamic-slice | bytes 12
  21.9 0.0 all-to-all-done.1
  21.9 5.1 %all-to-all-start = ((f32[8,16,512]{2,1,0:T(8,128)}), f32[8,16,512]{2,1,0:T(8,128)S(1)}, u32[]{:S(2)}, u32[]{:S(2)}) async-start(f32[8,16,512]{2,1,0:T(8,128)} %get-tuple-element.20), calls=%async_computation | async-start | bytes 524288 | tf_op jit(solution)/shard_map/all_to_all | solution.py:72
  27.1 0.2 add_dynamic-update-slice_fusion
  27.2 7.4 %all-reduce = s32[384]{0:T(512)S(1)} all-reduce(s32[384]{0:T(512)S(1)} %add_dynamic-update-slice_fusion), channel_id=1, replica_groups=mesh['region'=8,'state'=4] {'state'}, use_global_device_ids=true, to_apply=%add | all-reduce | flops 384 | bytes 3072
  34.6 0.8 %select_multiply_fusion = f32[256,384]{0,1:T(8,128)S(1)} fusion(s32[384]{0:T(512)S(1)} %get-tuple-element.18, s32[256]{0:T(256)S(1)} %get-tuple-element.23, s32[384]{0:T(512)S(1)} %get-tuple-element.17, s32[256]{0:T(256)S(1)} %get-tuple-element.24), kind=kLoop, calls=%fused_computation.12 | loop fusion | flops 4718592 | bytes 398336 | tf_op jit(solution)/shard_map/div | solution.py:41
  35.4 0.3 mul.120
  35.7 0.0 copy-start.1
  35.7 1.5 %copy.8 = f32[48,8,4,256]{3,1,2,0:T(8,128)} copy(f32[48,8,4,256]{3,2,1,0:T(4,128)S(1)} %bitcast.48) | data formatting | bytes 3145728
  37.2 0.0 all-to-all-done
  37.2 5.1 %all-to-all-start.2 = ((f32[8,16,512]{2,1,0:T(8,128)}), f32[8,16,512]{2,1,0:T(8,128)S(1)}, u32[]{:S(2)}, u32[]{:S(2)}) async-start(f32[8,16,512]{2,1,0:T(8,128)} %get-tuple-element.19), calls=%async_computation.2 | async-start | bytes 524288 | tf_op jit(solution)/shard_map/all_to_all | solution.py:75
  42.3 0.0 copy-done.1
  42.3 12.7 %all_gather.9 = f32[384,512]{1,0:T(8,128)S(1)} all-gather(f32[96,512]{1,0:T(8,128)S(1)} %pad_maximum_fusion), channel_id=1, replica_groups=mesh['region'=8,'state'=4] {'state'}, dimensions={0}, use_global_device_ids=true | all-gather | bytes 983040 | tf_op jit(solution)/shard_map/all_gather | solution.py:106
  55.0 0.0 copy-done
  55.0 5.3 %bitcast_multiply_fusion = f32[1024,384]{0,1:T(8,128)} fusion(f32[1024,384]{0,1:T(8,128)} %bitcast.47, f32[384,512]{1,0:T(8,128)S(1)} %all_gather.9, f32[1024,512]{1,0:T(8,128)S(1)} %bitcast.45), kind=kOutput, calls=%fused_computation.1 | convolution fusion | flops 2416312320 | bytes 6029312 | tf_op jit(solution)/shard_map/rm,pm->rp/dot_general | solution.py:38
  60.4 0.0 copy-start.2
  60.4 3.1 %copy.7 = f32[1024,384]{1,0:T(8,128)} copy(f32[1024,384]{0,1:T(8,128)} %bitcast_multiply_fusion) | data formatting | bytes 3145728 | tf_op jit(solution)/shard_map/reshape.79
  63.4 0.0 all-to-all-done.2
  63.4 0.0 copy-done.2
  63.5 10.1 %all_gather.11 = f32[384,512]{1,0:T(8,128)S(1)} all-gather(f32[96,512]{1,0:T(8,128)S(1)} %pad_maximum_fusion.1), channel_id=1, replica_groups=mesh['region'=8,'state'=4] {'state'}, dimensions={0}, use_global_device_ids=true | all-gather | bytes 983040 | tf_op jit(solution)/shard_map/all_gather | solution.py:107
  73.6 6.2 %convolution_bitcast_fusion = f32[1,4,256,512]{3,2,1,0:T(8,128)} fusion(f32[4,256,384]{2,1,0:T(8,128)} %bitcast.46, f32[384,512]{1,0:T(8,128)S(1)} %all_gather.11), kind=kOutput, calls=%fused_computation | convolution fusion | flops 2415919104 | bytes 4456448 | tf_op jit(solution)/shard_map/dot_general | solution.py:43
  (8 shorter events, 0.1 us)
Async XLA Ops:
  0.0 55.0 %copy-start = (f32[1,4,256,512]{3,2,1,0:T(8,128)S(1)}, f32[1,4,256,512]{3,2,1,0:T(8,128)}, u32[]{:S(2)}) copy-start(f32[1,4,256,512]{3,2,1,0:T(8,128)} %param.5) | copy-start | bytes 6291460
  7.4 14.5 %all-to-all-start.1 = ((s32[8,1,16]{2,1,0:T(1,128)}), s32[8,1,16]{2,1,0:T(1,128)S(1)}, u32[]{:S(2)}, u32[]{:S(2)}) async-start(s32[8,1,16]{2,1,0:T(1,128)} %fusion.8), calls=%async_computation.1 | async-start | bytes 8192 | tf_op jit(solution)/shard_map/all_to_all | solution.py:78
  21.9 15.3 %all-to-all-start = ((f32[8,16,512]{2,1,0:T(8,128)}), f32[8,16,512]{2,1,0:T(8,128)S(1)}, u32[]{:S(2)}, u32[]{:S(2)}) async-start(f32[8,16,512]{2,1,0:T(8,128)} %get-tuple-element.20), calls=%async_computation | async-start | bytes 524288 | tf_op jit(solution)/shard_map/all_to_all | solution.py:72
  35.7 6.6 %copy-start.1 = (f32[1,64,512]{2,1,0:T(8,128)S(1)}, f32[1,64,512]{2,1,0:T(8,128)}, u32[]{:S(2)}) copy-start(f32[1,64,512]{2,1,0:T(8,128)} %param.6) | copy-start | bytes 393220
  37.2 26.2 %all-to-all-start.2 = ((f32[8,16,512]{2,1,0:T(8,128)}), f32[8,16,512]{2,1,0:T(8,128)S(1)}, u32[]{:S(2)}, u32[]{:S(2)}) async-start(f32[8,16,512]{2,1,0:T(8,128)} %get-tuple-element.19), calls=%async_computation.2 | async-start | bytes 524288 | tf_op jit(solution)/shard_map/all_to_all | solution.py:75
  60.4 3.1 %copy-start.2 = (f32[1,64,512]{2,1,0:T(8,128)S(1)}, f32[1,64,512]{2,1,0:T(8,128)}, u32[]{:S(2)}) copy-start(f32[1,64,512]{2,1,0:T(8,128)} %param.7) | copy-start | bytes 393220
where the time goes:
time: 80.5 us; the launch traced here: 79.8 us
  blocking collectives  30.2 us (38%)
  starting transfers between devices  16.5 us (20%)
  matrix products  11.5 us (14%)
  other arithmetic  8.01 us (10%)
  local copies, waits for them, and re-layouts  7.03 us (9%)
  between operations  6.46 us (8%)
    all_gather x1, blocking collectives, on_device(): lax.all_gather(joined[0], 'state', axis=0, tiled=True)  12.7 us
    all_gather x1, blocking collectives, on_device(): lax.all_gather(joined[1], 'state', axis=0, tiled=True)  10.1 us
    unnamed x1, blocking collectives  7.37 us
    all_to_all x1, starting transfers between devices, on_device(): lax.all_to_all(place(low_set[2], high_set[2]), 'region', split_axis=0, co...  6.35 us
    dot_general x1, matrix products, add_block(): return jnp.dot(covar, piece_weight, precision=lax.Precision.HIGHEST)  6.17 us
    dot_general x1, matrix products, add_block(): jnp.einsum('rm,pm->rp', flat_state, piece_anom, precision=lax.Precision.H...  5.33 us
    all_to_all x1, starting transfers between devices, on_device(): lax.all_to_all(place(low_set[0], high_set[0]), 'region', split_axis=0, co...  5.11 us
    all_to_all x1, starting transfers between devices, on_device(): lax.all_to_all(place(low_set[1], high_set[1]), 'region', split_axis=0, co...  5.08 us
  transfers between devices with their start and end apart: 3, of which 0 were waited for; matrix products, arithmetic and copies ran while one was open for 19% of the time, Pallas kernels for 0%

commit v1 on v0

--- a/solution.py
+++ b/solution.py
@@ -2,12 +2,26 @@
 import jax.numpy as jnp
 from jax import lax
 from jax.sharding import PartitionSpec as P
+from jax.lax import axis_index, axis_size, ppermute
 
 SECT_W = 32
 LAT = 8
 HALF = 4
 CAP = 16
 COLS = 256
+
+
+def _draw_files(block_in, pos_dim, local):
+    met_up, outer = (block_in.shape[:pos_dim], block_in.shape[pos_dim + 1 :])
+    return jnp.moveaxis(block_in.reshape(*met_up, local, -1, *outer), pos_dim, 0)
+
+
+def view_teams_up(point, dim_at):
+    point = jnp.moveaxis(point, 0, dim_at)
+    a_next = point.shape
+    return point.reshape(
+        *a_next[:dim_at], a_next[dim_at] * a_next[dim_at + 1], *a_next[dim_at + 2 :]
+    )
 
 
 def gaspari(scaled):
@@ -68,6 +82,16 @@
             to_right.reshape(shaped), second[None], 0
         )
 
+    def _serve_turns(local_x, shard_axis, z, arr):
+        plain, newest = (axis_size(shard_axis), axis_index(shard_axis))
+        back = _draw_files(local_x, z, plain)
+        column = [back[newest]]
+        for at in range(1, plain):
+            s_next = back[newest ^ at]
+            column.append(ppermute(s_next, shard_axis, [(d, d ^ at) for d in range(plain)]))
+        back = jnp.stack(column)[newest ^ jnp.arange(plain)]
+        return view_teams_up(back, arr)
+
     slotted = (
         lax.all_to_all(
             place(low_set[0], high_set[0]), "region", split_axis=0, concat_axis=0, tiled=True
@@ -75,9 +99,7 @@
         lax.all_to_all(
             place(low_set[1], high_set[1]), "region", split_axis=0, concat_axis=0, tiled=True
         ),
-        lax.all_to_all(
-            place(low_set[2], high_set[2]), "region", split_axis=0, concat_axis=0, tiled=True
-        ),
+        _serve_turns(place(low_set[2], high_set[2]), "region", 0, 0),
     )
     from_left = tuple(
         (lax.dynamic_index_in_dim(pieces, left_region, 0, keepdims=False) for pieces in slotted)

time: 80.5 us -> 85.9 us (1.067)
  waiting for transfers between devices: 0.01 us -> 4.72 us
  starting transfers between devices: 16.5 us -> 18.2 us
  other arithmetic: 8.01 us -> 6.9 us
    ppermute x0 -> x7, starting transfers between devices: none -> 9.88 us  [_serve_turns(): ppermute(s_next, shard_axis, [(d, d ^ at) for d in range(plain)])]
    all_to_all x1 -> x0, starting transfers between devices: 6.35 us -> none  [on_device(): lax.all_to_all(place(low_set[2], high_set[2]), 'region', split_axis=0, co...]
    ppermute x0 -> x7, waiting for transfers between devices: none -> 4.71 us  [_serve_turns(): ppermute(s_next, shard_axis, [(d, d ^ at) for d in range(plain)])]
    all_to_all x1, starting transfers between devices: 5.08 us -> 3.41 us  [on_device(): lax.all_to_all(place(low_set[1], high_set[1]), 'region', split_axis=0, co...]
    unnamed x9 -> x20, local copies, waits for them, and re-layouts: 2.8 us -> 2.14 us
    another operation x1 -> x2, local copies, waits for them, and re-layouts: 3.06 us -> 3.09 us
  transfers between devices with their start and end apart: 3 -> 9, of which waited for: 0 -> 2; matrix products, arithmetic and copies ran while one was open for 19% -> 17% of each run, Pallas kernels for 0% -> 0%
where the time goes in v1:
time: 85.9 us; the launch traced here: 85.3 us
  blocking collectives  30 us (35%)
  starting transfers between devices  18.2 us (21%)
  matrix products  11.5 us (13%)
  local copies, waits for them, and re-layouts  6.99 us (8%)
  between operations  6.94 us (8%)
  other arithmetic  6.9 us (8%)
  waiting for transfers between devices  4.72 us (5%)
    all_gather x1, blocking collectives, on_device(): lax.all_gather(joined[0], 'state', axis=0, tiled=True)  12.5 us
    all_gather x1, blocking collectives, on_device(): lax.all_gather(joined[1], 'state', axis=0, tiled=True)  10.1 us
    ppermute x7, starting transfers between devices, _serve_turns(): ppermute(s_next, shard_axis, [(d, d ^ at) for d in range(plain)])  9.88 us
    unnamed x1, blocking collectives  7.37 us
    dot_general x1, matrix products, add_block(): return jnp.dot(covar, piece_weight, precision=lax.Precision.HIGHEST)  6.17 us
    dot_general x1, matrix products, add_block(): jnp.einsum('rm,pm->rp', flat_state, piece_anom, precision=lax.Precision.H...  5.32 us
    all_to_all x1, starting transfers between devices, on_device(): lax.all_to_all(place(low_set[0], high_set[0]), 'region', split_axis=0, co...  4.93 us
    ppermute x7, waiting for transfers between devices, _serve_turns(): ppermute(s_next, shard_axis, [(d, d ^ at) for d in range(plain)])  4.71 us
  transfers between devices with their start and end apart: 9, of which 2 were waited for; matrix products, arithmetic and copies ran while one was open for 17% of the time, Pallas kernels for 0%

profile of v1, /device:TPU:0, one launch (start us, length us, event | category | flops | bytes accessed | tf_op | source)
XLA Modules:
  0.0 85.3 jit_solution(893192542283246066)
XLA Ops:
  0.0 0.0 copy-start
  0.0 0.0 copy-start.4
  0.0 0.0 copy-start.3
  0.0 1.5 %fusion.10 = s32[]{:T(128)} fusion(s32[8]{0:T(128)} %param.9, s32[]{:T(128)S(6)} %axis_index.19), kind=kLoop, calls=%fused_computation.70 | loop fusion | flops 23 | bytes 40 | tf_op jit(solution)/shard_map/reduce_sum | solution.py:65
  3.5 0.7 broadcast_add_fusion
  4.1 0.1 slice_bitcast_fusion.5
  4.2 1.4 %fusion.11 = (s32[]{:T(128)}, s32[]{:T(128)}) fusion(s32[8]{0:T(128)} %param.9, s32[]{:T(128)S(6)} %select_n.144, s32[]{:T(128)S(6)} %select_n.147), kind=kLoop, calls=%fused_computation.71 | loop fusion | flops 46 | bytes 48 | tf_op jit(solution)/shard_map/reduce_sum | solution.py:66
  5.6 1.3 %iota_compare_fusion = (pred[8]{0:T(512)(128)(4,1)S(1)}, pred[8]{0:T(512)(128)(4,1)S(1)}) fusion(s32[]{:T(128)} %get-tuple-element.6, s32[]{:T(128)} %get-tuple-element.5), kind=kLoop, calls=%fused_computation.81 | loop fusion | flops 16 | bytes 24 | tf_op jit(solution)/shard_map/eq | solution.py:77
  7.0 0.1 select_add_fusion.2
  7.1 0.6 collective-permute-start
  7.6 2.6 %collective-permute-start.1 = (s32[1,16]{1,0:T(1,128)S(1)}, s32[1,16]{1,0:T(1,128)S(1)}, u32[]{:S(2)}, u32[]{:S(2)}) collective-permute-start(s32[1,16]{1,0:T(1,128)S(1)} %get-tuple-element.22), channel_id=1, source_target_pairs={{0,8},{4,12},{8,0},{12,4},{16,24},{20,28},{24,16},{28,20},{1,9},{5... | collective-permute-start | bytes 200 | tf_op jit(solution)/shard_map/ppermute | solution.py:91
  10.3 0.0 collective-permute-start.2
  10.3 2.8 %collective-permute-start.3 = (s32[1,16]{1,0:T(1,128)S(1)}, s32[1,16]{1,0:T(1,128)S(1)}, u32[]{:S(2)}, u32[]{:S(2)}) collective-permute-start(s32[1,16]{1,0:T(1,128)S(1)} %get-tuple-element.20), channel_id=1, source_target_pairs={{0,16},{4,20},{8,24},{12,28},{16,0},{20,4},{24,8},{28,12},{1,17},{... | collective-permute-start | bytes 200 | tf_op jit(solution)/shard_map/ppermute | solution.py:91
  13.1 0.0 collective-permute-start.4
  13.1 0.8 slice_bitcast_fusion.1
  13.9 0.9 %select_add_fusion = (f32[8,16,512]{2,1,0:T(8,128)}, f32[8,16,512]{2,1,0:T(8,128)}) fusion(f32[16,512]{1,0:T(8,128)S(1)} %get-tuple-element.12, f32[16,512]{1,0:T(8,128)S(1)} %get-tuple-element.11, pred[8]{0:T(512)(128)(4,1)S(1)} %get-tuple-element.32, pred[8]{0:T(512)(128)(4,1)S(1)} %get-tuple-element.33, f32[16,512]{1,0:T(8,128)S(1)} %get-tuple-element.34, ...), kind=kLoop, calls=%fused_computation.19 | loop fusion | flops 393216 | bytes 655376 | tf_op jit(solution)/shard_map/add | solution.py:81
  14.8 4.9 %all-to-all-start = ((f32[8,16,512]{2,1,0:T(8,128)}), f32[8,16,512]{2,1,0:T(8,128)S(1)}, u32[]{:S(2)}, u32[]{:S(2)}) async-start(f32[8,16,512]{2,1,0:T(8,128)} %get-tuple-element.27), calls=%async_computation | async-start | bytes 524288 | tf_op jit(solution)/shard_map/all_to_all | solution.py:96
  22.4 0.0 copy-done.3
  23.9 0.0 copy-done.4
  23.9 0.6 dynamic-slice.15
  25.1 0.0 collective-permute-done
  25.1 3.9 %collective-permute-start.5 = (s32[1,16]{1,0:T(1,128)S(1)}, s32[1,16]{1,0:T(1,128)S(1)}, u32[]{:S(2)}, u32[]{:S(2)}) collective-permute-start(s32[1,16]{1,0:T(1,128)S(1)} %get-tuple-element.18), channel_id=1, source_target_pairs={{0,24},{4,28},{8,16},{12,20},{16,8},{20,12},{24,0},{28,4},{1,25},{... | collective-permute-start | bytes 200 | tf_op jit(solution)/shard_map/ppermute | solution.py:91
  29.0 0.0 collective-permute-done.1
  29.0 0.0 collective-permute-start.6
  29.0 0.0 collective-permute-done.2
  29.1 0.0 collective-permute-done.3
  29.1 0.0 collective-permute-done.4
  29.1 1.5 %collective-permute-done.5 = s32[1,16]{1,0:T(1,128)S(1)} collective-permute-done((s32[1,16]{1,0:T(1,128)S(1)}, s32[1,16]{1,0:T(1,128)S(1)}, u32[]{:S(2)}, u32[]{:S(2)}) %collective-permute-start.5) | collective-permute-done | bytes 96 | tf_op jit(solution)/shard_map/ppermute | solution.py:91
  30.6 3.2 %collective-permute-done.6 = s32[1,16]{1,0:T(1,128)S(1)} collective-permute-done((s32[1,16]{1,0:T(1,128)S(1)}, s32[1,16]{1,0:T(1,128)S(1)}, u32[]{:S(2)}, u32[]{:S(2)}) %collective-permute-start.6) | collective-permute-done | bytes 96 | tf_op jit(solution)/shard_map/ppermute | solution.py:91
  33.8 0.6 gather_fusion
  34.4 0.2 add_dynamic-update-slice_fusion
  34.6 7.4 %all-reduce = s32[384]{0:T(512)S(1)} all-reduce(s32[384]{0:T(512)S(1)} %add_dynamic-update-slice_fusion), channel_id=1, replica_groups=mesh['region'=8,'state'=4] {'state'}, use_global_device_ids=true, to_apply=%add | all-reduce | flops 384 | bytes 3072
  42.0 0.8 select_multiply_fusion
  42.8 0.3 mul.120
  43.1 0.0 copy-start.1
  43.1 1.5 %copy.8 = f32[48,8,4,256]{3,1,2,0:T(8,128)} copy(f32[48,8,4,256]{3,2,1,0:T(4,128)S(1)} %bitcast.69) | data formatting | bytes 3145728
  44.5 0.0 all-to-all-done
  44.5 3.4 %all-to-all-start.1 = ((f32[8,16,512]{2,1,0:T(8,128)}), f32[8,16,512]{2,1,0:T(8,128)S(1)}, u32[]{:S(2)}, u32[]{:S(2)}) async-start(f32[8,16,512]{2,1,0:T(8,128)} %get-tuple-element.26), calls=%async_computation.1 | async-start | bytes 524288 | tf_op jit(solution)/shard_map/all_to_all | solution.py:99
  48.0 0.0 copy-done.1
  48.0 12.5 %all_gather.9 = f32[384,512]{1,0:T(8,128)S(1)} all-gather(f32[96,512]{1,0:T(8,128)S(1)} %pad_maximum_fusion), channel_id=1, replica_groups=mesh['region'=8,'state'=4] {'state'}, dimensions={0}, use_global_device_ids=true | all-gather | bytes 983040 | tf_op jit(solution)/shard_map/all_gather | solution.py:128
  60.5 0.0 copy-done
  60.5 5.3 %bitcast_multiply_fusion = f32[1024,384]{0,1:T(8,128)} fusion(f32[1024,384]{0,1:T(8,128)} %bitcast.68, f32[384,512]{1,0:T(8,128)S(1)} %all_gather.9, f32[1024,512]{1,0:T(8,128)S(1)} %bitcast.66), kind=kOutput, calls=%fused_computation.2 | convolution fusion | flops 2416312320 | bytes 6029312 | tf_op jit(solution)/shard_map/rm,pm->rp/dot_general | solution.py:52
  65.8 0.0 copy-start.2
  65.8 3.1 %copy.7 = f32[1024,384]{1,0:T(8,128)} copy(f32[1024,384]{0,1:T(8,128)} %bitcast_multiply_fusion) | data formatting | bytes 3145728 | tf_op jit(solution)/shard_map/reshape.75
  68.9 0.0 all-to-all-done.1
  68.9 0.0 copy-done.2
  69.0 10.1 %all_gather.11 = f32[384,512]{1,0:T(8,128)S(1)} all-gather(f32[96,512]{1,0:T(8,128)S(1)} %pad_maximum_fusion.1), channel_id=1, replica_groups=mesh['region'=8,'state'=4] {'state'}, dimensions={0}, use_global_device_ids=true | all-gather | bytes 983040 | tf_op jit(solution)/shard_map/all_gather | solution.py:129
  79.1 6.2 %convolution_bitcast_fusion = f32[1,4,256,512]{3,2,1,0:T(8,128)} fusion(f32[4,256,384]{2,1,0:T(8,128)} %bitcast.67, f32[384,512]{1,0:T(8,128)S(1)} %all_gather.11), kind=kOutput, calls=%fused_computation.1 | convolution fusion | flops 2415919104 | bytes 4456448 | tf_op jit(solution)/shard_map/dot_general | solution.py:57
  (20 shorter events, 0.2 us)
Async XLA Ops:
  0.0 60.5 %copy-start = (f32[1,4,256,512]{3,2,1,0:T(8,128)S(1)}, f32[1,4,256,512]{3,2,1,0:T(8,128)}, u32[]{:S(2)}) copy-start(f32[1,4,256,512]{3,2,1,0:T(8,128)} %param.5) | copy-start | bytes 6291460
  0.0 23.9 %copy-start.4 = (u32[32]{0:T(128)S(1)}, u32[32]{0:T(128)}, u32[]{:S(2)}) copy-start(u32[32]{0:T(128)} %constant.157) | copy-start | bytes 388
  0.0 22.4 %copy-start.3 = (s32[1,64]{1,0:T(1,128)S(1)}, s32[1,64]{1,0:T(1,128)}, u32[]{:S(2)}) copy-start(s32[1,64]{1,0:T(1,128)} %param.8) | copy-start | bytes 772
  7.1 18.0 %collective-permute-start = (s32[1,16]{1,0:T(1,128)S(1)}, s32[1,16]{1,0:T(1,128)S(1)}, u32[]{:S(2)}, u32[]{:S(2)}) collective-permute-start(s32[1,16]{1,0:T(1,128)S(1)} %get-tuple-element.23), channel_id=1, source_target_pairs={{0,4},{4,0},{8,12},{12,8},{16,20},{20,16},{24,28},{28,24},{1,5},{5... | collective-permute-start | bytes 200 | tf_op jit(solution)/shard_map/ppermute | solution.py:91
  7.6 21.4 %collective-permute-start.1 = (s32[1,16]{1,0:T(1,128)S(1)}, s32[1,16]{1,0:T(1,128)S(1)}, u32[]{:S(2)}, u32[]{:S(2)}) collective-permute-start(s32[1,16]{1,0:T(1,128)S(1)} %get-tuple-element.22), channel_id=1, source_target_pairs={{0,8},{4,12},{8,0},{12,4},{16,24},{20,28},{24,16},{28,20},{1,9},{5... | collective-permute-start | bytes 200 | tf_op jit(solution)/shard_map/ppermute | solution.py:91
  10.3 18.8 %collective-permute-start.2 = (s32[1,16]{1,0:T(1,128)S(1)}, s32[1,16]{1,0:T(1,128)S(1)}, u32[]{:S(2)}, u32[]{:S(2)}) collective-permute-start(s32[1,16]{1,0:T(1,128)S(1)} %get-tuple-element.21), channel_id=1, source_target_pairs={{0,12},{4,8},{8,4},{12,0},{16,28},{20,24},{24,20},{28,16},{1,13},{... | collective-permute-start | bytes 200 | tf_op jit(solution)/shard_map/ppermute | solution.py:91
  10.3 18.7 %collective-permute-start.3 = (s32[1,16]{1,0:T(1,128)S(1)}, s32[1,16]{1,0:T(1,128)S(1)}, u32[]{:S(2)}, u32[]{:S(2)}) collective-permute-start(s32[1,16]{1,0:T(1,128)S(1)} %get-tuple-element.20), channel_id=1, source_target_pairs={{0,16},{4,20},{8,24},{12,28},{16,0},{20,4},{24,8},{28,12},{1,17},{... | collective-permute-start | bytes 200 | tf_op jit(solution)/shard_map/ppermute | solution.py:91
  13.1 16.0 %collective-permute-start.4 = (s32[1,16]{1,0:T(1,128)S(1)}, s32[1,16]{1,0:T(1,128)S(1)}, u32[]{:S(2)}, u32[]{:S(2)}) collective-permute-start(s32[1,16]{1,0:T(1,128)S(1)} %get-tuple-element.19), channel_id=1, source_target_pairs={{0,20},{4,16},{8,28},{12,24},{16,4},{20,0},{24,12},{28,8},{1,21},{... | collective-permute-start | bytes 200 | tf_op jit(solution)/shard_map/ppermute | solution.py:91
  14.8 29.7 %all-to-all-start = ((f32[8,16,512]{2,1,0:T(8,128)}), f32[8,16,512]{2,1,0:T(8,128)S(1)}, u32[]{:S(2)}, u32[]{:S(2)}) async-start(f32[8,16,512]{2,1,0:T(8,128)} %get-tuple-element.27), calls=%async_computation | async-start | bytes 524288 | tf_op jit(solution)/shard_map/all_to_all | solution.py:96
  25.1 5.4 %collective-permute-start.5 = (s32[1,16]{1,0:T(1,128)S(1)}, s32[1,16]{1,0:T(1,128)S(1)}, u32[]{:S(2)}, u32[]{:S(2)}) collective-permute-start(s32[1,16]{1,0:T(1,128)S(1)} %get-tuple-element.18), channel_id=1, source_target_pairs={{0,24},{4,28},{8,16},{12,20},{16,8},{20,12},{24,0},{28,4},{1,25},{... | collective-permute-start | bytes 200 | tf_op jit(solution)/shard_map/ppermute | solution.py:91
  29.0 4.8 %collective-permute-start.6 = (s32[1,16]{1,0:T(1,128)S(1)}, s32[1,16]{1,0:T(1,128)S(1)}, u32[]{:S(2)}, u32[]{:S(2)}) collective-permute-start(s32[1,16]{1,0:T(1,128)S(1)} %get-tuple-element.17), channel_id=1, source_target_pairs={{0,28},{4,24},{8,20},{12,16},{16,12},{20,8},{24,4},{28,0},{1,29},{... | collective-permute-start | bytes 200 | tf_op jit(solution)/shard_map/ppermute | solution.py:91
  43.1 4.9 %copy-start.1 = (f32[1,64,512]{2,1,0:T(8,128)S(1)}, f32[1,64,512]{2,1,0:T(8,128)}, u32[]{:S(2)}) copy-start(f32[1,64,512]{2,1,0:T(8,128)} %param.6) | copy-start | bytes 393220
  44.5 24.4 %all-to-all-start.1 = ((f32[8,16,512]{2,1,0:T(8,128)}), f32[8,16,512]{2,1,0:T(8,128)S(1)}, u32[]{:S(2)}, u32[]{:S(2)}) async-start(f32[8,16,512]{2,1,0:T(8,128)} %get-tuple-element.26), calls=%async_computation.1 | async-start | bytes 524288 | tf_op jit(solution)/shard_map/all_to_all | solution.py:99
  65.8 3.1 %copy-start.2 = (f32[1,64,512]{2,1,0:T(8,128)S(1)}, f32[1,64,512]{2,1,0:T(8,128)}, u32[]{:S(2)}) copy-start(f32[1,64,512]{2,1,0:T(8,128)} %param.7) | copy-start | bytes 393220
